TPU v7x, 256 devices: a whole 4x4x8 slice. The times are simulated.
256 devices in a mesh: chan: 32 (over y_lo, z, core), tm: 8 (over y_hi, x).
Axes of the slice: x: 4, y: 4 (y_hi: 2, y_lo: 2; y = y_hi * 2 + y_lo), z: 8, core: 2. Of those that a mesh axis runs over, the one named last changes fastest.
Arguments:
- traces: bfloat16 [256, 6144], P('chan', 'tm'), may hold values from -6 to 6
- validity: int32 [256], P('chan'), may hold values 0 or 1
- owners: int32 [8], replicated, may hold values from 0 to 31
Outputs:
- correlations: float32 [8, 256, 8, 2048], P(None, 'chan', None, 'tm')
All inputs are finite; a program needn't handle non-finite values. No bound on the sum of `validity` on one device may be relied on, other than what follows from the above.
Results may differ from a plain program's by a relative error of at most 0.0003.
Values may be sent and summed in bfloat16 or wider, within the bound.
No kernel may reach another device: no remote copies, remote signals or barrier semaphores. Data moves between devices by JAX's collectives and lax.ppermute only.
A program may use at most 64 MiB of HBM per device.

v0:
```python
import math

import jax
import jax.numpy as jnp
from jax import lax
from jax.sharding import PartitionSpec as P

LAG = 1024


def broadcast(block, axis, holder):
    block = jnp.where(lax.axis_index(axis) == holder, block, jnp.zeros_like(block))
    return lax.psum(block, axis)


def toeplitz(segment, lag_rows, time_cols):
    seg_width = segment.shape[1]
    repeated = jnp.tile(segment, (1, lag_rows + 1))[:, : lag_rows * (seg_width + 1)]
    return repeated.reshape(segment.shape[0], lag_rows, seg_width + 1)[:, :, :time_cols]


def on_device(traces, validity, owners):
    channels_here = traces.shape[0]
    step_count = owners.shape[0]
    receiver = lax.all_gather(traces, "tm", axis=1, tiled=True)
    time_len = receiver.shape[1]
    lag_dev = 2 * LAG // lax.axis_size("tm")
    valid_flags = validity.astype(jnp.bfloat16)

    def fetch_piece(step_number, buffers):
        source_pieces, source_flags = buffers
        fetched, fetched_flags = (
            broadcast(traces, "chan", owners[step_number]),
            broadcast(valid_flags, "chan", owners[step_number]),
        )
        return (
            source_pieces.at[step_number].set(fetched),
            source_flags.at[step_number].set(fetched_flags),
        )

    initial = (
        jnp.zeros((step_count,) + traces.shape, jnp.bfloat16),
        jnp.zeros((step_count, channels_here), jnp.bfloat16),
    )
    source_pieces, source_flags = lax.fori_loop(0, step_count, fetch_piece, initial)
    sources = lax.all_gather(source_pieces, "tm", axis=2, tiled=True)
    padded = jnp.pad(receiver, ((0, 0), (LAG, LAG)))
    offset = lax.axis_index("tm") * lag_dev
    block_len = 512

    def accumulate(block_number, summed):
        begin_at = block_number * block_len
        segment = lax.dynamic_slice_in_dim(padded, begin_at + offset, block_len + lag_dev, 1)
        shifted = toeplitz(segment, lag_dev, block_len)
        source_block = lax.dynamic_slice_in_dim(sources, begin_at, block_len, 2)
        return summed + jnp.einsum(
            "rku,scu->srck", shifted, source_block, preferred_element_type=jnp.float32
        )

    zeros_acc = jnp.zeros((step_count, channels_here, channels_here, lag_dev), jnp.float32)
    summed = lax.fori_loop(0, time_len // block_len, accumulate, zeros_acc)
    pair_weight = (
        validity.astype(jnp.float32)[None, :, None, None]
        * source_flags.astype(jnp.float32)[:, None, :, None]
    )
    return summed * (1.0 / math.sqrt(time_len)) * pair_weight


def solution(mesh):
    placed = (P("chan", "tm"), P("chan"), P())
    return jax.shard_map(
        on_device,
        mesh=mesh,
        in_specs=placed,
        out_specs=P(None, "chan", None, "tm"),
        check_vma=False,
    )
```

profile of v0, /device:TPU:1, one launch (start us, length us, event | category | flops | bytes accessed | tf_op | source)
XLA Modules:
  0.0 1197.2 jit_solution(13575276252941144519)
XLA Ops:
  0.8 888.7 %while.31 = (s32[]{:T(128)}, bf16[8,8,768]{2,1,0:T(8,128)(2,1)S(1)}, bf16[8,8]{1,0:T(8,128)(2,1)S(1)}, s32[8]{0:T(128)}, bf16[8,768]{1,0:T(8,128)(2,1)}, /*index...) while((s32[]{:T(128)}, ...), condition=%wide.region_5.6_spmd, body=%wide.region_0.5_spmd.sunk | while | flops 18488 | bytes 86400 | solution.py:45
  2.7 107.8 %all-reduce.3 = (bf16[1,8,768]{2,1,0:T(8,128)(2,1)S(1)}, bf16[1,8]{1,0:T(2,128)(2,1)S(1)}) all-reduce(bf16[1,8,768]{2,1,0:T(8,128)(2,1)S(1)} %select_bitcast_fusion.2, bf16[1,8]{1,0:T(2,128)(2,1)S(1)} %fusion.11), channel_id=1, replica_groups=mesh['chan'=32,'tm'=8] {'chan'}, use_global_device_ids=true, to_apply=%region_2.2 | all-reduce | flops 6152 | bytes 24608 | tf_op jit(solution)/shard_map/while/body/eval_jaxpr/psum | solution.py:13
  116.6 104.5 %all-reduce.3 = (bf16[1,8,768]{2,1,0:T(8,128)(2,1)S(1)}, bf16[1,8]{1,0:T(2,128)(2,1)S(1)}) all-reduce(bf16[1,8,768]{2,1,0:T(8,128)(2,1)S(1)} %select_bitcast_fusion.2, bf16[1,8]{1,0:T(2,128)(2,1)S(1)} %fusion.11), channel_id=1, replica_groups=mesh['chan'=32,'tm'=8] {'chan'}, use_global_device_ids=true, to_apply=%region_2.2 | all-reduce | flops 6152 | bytes 24608 | tf_op jit(solution)/shard_map/while/body/eval_jaxpr/psum | solution.py:13
  227.2 104.6 %all-reduce.3 = (bf16[1,8,768]{2,1,0:T(8,128)(2,1)S(1)}, bf16[1,8]{1,0:T(2,128)(2,1)S(1)}) all-reduce(bf16[1,8,768]{2,1,0:T(8,128)(2,1)S(1)} %select_bitcast_fusion.2, bf16[1,8]{1,0:T(2,128)(2,1)S(1)} %fusion.11), channel_id=1, replica_groups=mesh['chan'=32,'tm'=8] {'chan'}, use_global_device_ids=true, to_apply=%region_2.2 | all-reduce | flops 6152 | bytes 24608 | tf_op jit(solution)/shard_map/while/body/eval_jaxpr/psum | solution.py:13
  337.8 104.5 %all-reduce.3 = (bf16[1,8,768]{2,1,0:T(8,128)(2,1)S(1)}, bf16[1,8]{1,0:T(2,128)(2,1)S(1)}) all-reduce(bf16[1,8,768]{2,1,0:T(8,128)(2,1)S(1)} %select_bitcast_fusion.2, bf16[1,8]{1,0:T(2,128)(2,1)S(1)} %fusion.11), channel_id=1, replica_groups=mesh['chan'=32,'tm'=8] {'chan'}, use_global_device_ids=true, to_apply=%region_2.2 | all-reduce | flops 6152 | bytes 24608 | tf_op jit(solution)/shard_map/while/body/eval_jaxpr/psum | solution.py:13
  448.4 105.2 %all-reduce.3 = (bf16[1,8,768]{2,1,0:T(8,128)(2,1)S(1)}, bf16[1,8]{1,0:T(2,128)(2,1)S(1)}) all-reduce(bf16[1,8,768]{2,1,0:T(8,128)(2,1)S(1)} %select_bitcast_fusion.2, bf16[1,8]{1,0:T(2,128)(2,1)S(1)} %fusion.11), channel_id=1, replica_groups=mesh['chan'=32,'tm'=8] {'chan'}, use_global_device_ids=true, to_apply=%region_2.2 | all-reduce | flops 6152 | bytes 24608 | tf_op jit(solution)/shard_map/while/body/eval_jaxpr/psum | solution.py:13
  559.7 104.6 %all-reduce.3 = (bf16[1,8,768]{2,1,0:T(8,128)(2,1)S(1)}, bf16[1,8]{1,0:T(2,128)(2,1)S(1)}) all-reduce(bf16[1,8,768]{2,1,0:T(8,128)(2,1)S(1)} %select_bitcast_fusion.2, bf16[1,8]{1,0:T(2,128)(2,1)S(1)} %fusion.11), channel_id=1, replica_groups=mesh['chan'=32,'tm'=8] {'chan'}, use_global_device_ids=true, to_apply=%region_2.2 | all-reduce | flops 6152 | bytes 24608 | tf_op jit(solution)/shard_map/while/body/eval_jaxpr/psum | solution.py:13
  670.3 104.5 %all-reduce.3 = (bf16[1,8,768]{2,1,0:T(8,128)(2,1)S(1)}, bf16[1,8]{1,0:T(2,128)(2,1)S(1)}) all-reduce(bf16[1,8,768]{2,1,0:T(8,128)(2,1)S(1)} %select_bitcast_fusion.2, bf16[1,8]{1,0:T(2,128)(2,1)S(1)} %fusion.11), channel_id=1, replica_groups=mesh['chan'=32,'tm'=8] {'chan'}, use_global_device_ids=true, to_apply=%region_2.2 | all-reduce | flops 6152 | bytes 24608 | tf_op jit(solution)/shard_map/while/body/eval_jaxpr/psum | solution.py:13
  780.9 104.5 %all-reduce.3 = (bf16[1,8,768]{2,1,0:T(8,128)(2,1)S(1)}, bf16[1,8]{1,0:T(2,128)(2,1)S(1)}) all-reduce(bf16[1,8,768]{2,1,0:T(8,128)(2,1)S(1)} %select_bitcast_fusion.2, bf16[1,8]{1,0:T(2,128)(2,1)S(1)} %fusion.11), channel_id=1, replica_groups=mesh['chan'=32,'tm'=8] {'chan'}, use_global_device_ids=true, to_apply=%region_2.2 | all-reduce | flops 6152 | bytes 24608 | tf_op jit(solution)/shard_map/while/body/eval_jaxpr/psum | solution.py:13
  889.5 32.3 %all_gather.6 = bf16[8,8,6144]{2,1,0:T(8,128)(2,1)} all-gather(bf16[8,8,768]{2,1,0:T(8,128)(2,1)S(1)} %get-tuple-element.253), channel_id=1, replica_groups=mesh['chan'=32,'tm'=8] {'tm'}, dimensions={2}, use_global_device_ids=true | all-gather | bytes 884736 | tf_op jit(solution)/shard_map/all_gather | solution.py:46
  921.8 28.4 %all_gather.7 = bf16[8,6144]{1,0:T(8,128)(2,1)S(1)} all-gather(bf16[8,768]{1,0:T(8,128)(2,1)} %get-tuple-element.441), channel_id=1, replica_groups=mesh['chan'=32,'tm'=8] {'tm'}, dimensions={1}, use_global_device_ids=true | all-gather | bytes 110592 | tf_op jit(solution)/shard_map/all_gather | solution.py:25
  950.3 244.9 %while.32 = (s32[]{:T(128)}, f32[8,8,8,256]{3,2,1,0:T(8,128)}, bf16[8,8,6144]{2,1,0:T(8,128)(2,1)}, s32[]{:T(128)}, bf16[8,8192]{1,0:T(8,128)(2,1)S(1)}, /*index...) while((s32[]{:T(128)}, f32[8,8,8,256]{3,2,1,0:T(8,128)}, ...), condition=%wide.region_7.8_spmd.clone, body=%wide.region_6.7_spmd.clone.sunk | while | flops 134479888 | bytes 29499664 | solution.py:61
  957.2 10.3 reshape.131
  977.6 10.3 reshape.131
  998.0 10.3 reshape.131
  1018.4 10.3 reshape.131
  1038.8 10.3 reshape.131
  1059.2 10.3 reshape.131
  1079.6 10.3 reshape.131
  1100.0 10.3 reshape.131
  1120.4 10.3 reshape.131
  1140.8 10.3 reshape.131
  1161.2 10.3 reshape.131
  1181.6 10.3 reshape.131
  (180 shorter events, 167.0 us)
Async XLA Ops:
  957.2 10.3 copy-start
  969.9 0.8 copy-start.1
  977.6 10.3 copy-start
  990.3 0.8 copy-start.1
  998.0 10.3 copy-start
  1010.7 0.8 copy-start.1
  1018.4 10.3 copy-start
  1031.1 0.8 copy-start.1
  1038.8 10.3 copy-start
  1051.5 0.8 copy-start.1
  1059.2 10.3 copy-start
  1071.9 0.8 copy-start.1
  1079.6 10.3 copy-start
  1092.3 0.8 copy-start.1
  1100.0 10.3 copy-start
  1112.7 0.8 copy-start.1
  1120.4 10.3 copy-start
  1133.1 0.8 copy-start.1
  1140.8 10.3 copy-start
  1153.6 0.8 copy-start.1
  1161.2 10.3 copy-start
  1174.0 0.8 copy-start.1
  1181.6 10.3 copy-start
  1194.4 0.8 copy-start.1
where the time goes:
time: 1210 us; the launch traced here: 1200 us
  blocking collectives  901 us (74%)
  local copies, waits for them, and re-layouts  226 us (19%)
  other arithmetic  35.6 us (3%)
  matrix products  29.5 us (2%)
    psum x8, blocking collectives, broadcast(): return lax.psum(block, axis)  840 us
    reshape x12, local copies, waits for them, and re-layouts, toeplitz(): repeated.reshape(segment.shape[0], lag_rows, seg_width + 1)  123 us
    while x60, local copies, waits for them, and re-layouts  86 us
    all_gather x1, blocking collectives, on_device(): sources = lax.all_gather(source_pieces, 'tm', axis=2, tiled=True)  32.3 us
    dot_general x12, matrix products, accumulate(): jnp.einsum('rku,scu->srck', shifted, source_block, preferred_element_type...  29.5 us
    all_gather x1, blocking collectives, on_device(): receiver = lax.all_gather(traces, 'tm', axis=1, tiled=True)  28.4 us
    another operation x40, other arithmetic  27.6 us

commit v1 on v0

v1 whole, which is shorter than its diff:
```python
import math

import jax
import jax.numpy as jnp
from jax import lax
from jax.experimental import pallas as pl
from jax.experimental.pallas import tpu as pltpu
from jax.sharding import Mesh, PartitionSpec as P

LAG = 1024
TIME = 6144
PIECE = 768
HALF = 384
FINE = 32
DEPTH = 6400
NAMES = ("y_lo", "z", "core", "y_hi", "x")
CHAN = ("y_lo", "z", "core")
TM = ("y_hi", "x")


def pick_kernel(owners_ref, row_ref, gathered_ref, out_ref):
    mine = row_ref[0]
    rows = [mine] + [owners_ref[s] for s in range(8)] + [mine + 1 - 2 * (mine % 2)]
    for place, row in enumerate(rows):
        block = gathered_ref[row]
        for peer in range(8):
            out_ref[peer, 8 * place : 8 * place + 8, :] = block


def pick(owners, row, gathered):
    return pl.pallas_call(
        pick_kernel,
        out_shape=jax.ShapeDtypeStruct((8, 80, HALF), jnp.bfloat16),
        in_specs=[pl.BlockSpec(memory_space=pltpu.SMEM)] * 2 + [pl.BlockSpec(memory_space=pltpu.VMEM)],
        out_specs=pl.BlockSpec(memory_space=pltpu.VMEM),
        compiler_params=pltpu.CompilerParams(vmem_limit_bytes=4 << 20),
    )(owners, row, gathered)


def corr_kernel(place_ref, own_ref, other_ref, out_ref, rec_ref, src_ref, h_ref):
    core = place_ref[0]
    m = place_ref[1]
    f32, bf16 = jnp.float32, jnp.bfloat16
    rec_ref[:, :LAG] = jnp.zeros((8, LAG), f32)
    rec_ref[:, LAG + TIME :] = jnp.zeros((8, rec_ref.shape[1] - LAG - TIME), f32)
    src_ref[:, :128] = jnp.zeros((256, 128), bf16)
    src_ref[:, 128 + TIME :] = jnp.zeros((256, src_ref.shape[1] - 128 - TIME), bf16)
    for piece in range(8):
        for ref, half, row in ((own_ref, core, 0), (other_ref, 1 - core, 72)):
            at = pl.multiple_of(PIECE * piece + HALF * half, 128)
            rec_ref[:, pl.ds(LAG + at, HALF)] = ref[piece, row : row + 8, :].astype(f32)
            src_ref[:64, pl.ds(128 + at, HALF)] = ref[piece, 8:72, :]
    lane = lax.broadcasted_iota(jnp.int32, (64, 128), 1)
    before = [None] * 4
    for k in range(src_ref.shape[1] // 128):
        tile = src_ref[:64, k * 128 : (k + 1) * 128].astype(f32)
        for i in range(1, 4):
            turned = pltpu.roll(tile, FINE * i, 1)
            if before[i] is not None:
                src_ref[64 * i : 64 * i + 64, k * 128 : (k + 1) * 128] = jnp.where(
                    lane < FINE * i, before[i], turned
                ).astype(bf16)
            before[i] = turned
    base = pl.multiple_of(256 * m, 128)
    lane32 = lax.broadcasted_iota(jnp.int32, (FINE, 128), 1)
    row32 = lax.broadcasted_iota(jnp.int32, (FINE, 128), 0)
    cross = lane32 + (FINE - 1) - row32 >= 128
    for r in range(8):
        last = None
        for k in range(DEPTH // 128 + 1):
            wide = jnp.broadcast_to(rec_ref[r : r + 1, pl.ds(base + k * 128, 128)], (FINE, 128))
            turned = pltpu.roll(wide, 128 - (FINE - 1), 1, stride=1, stride_axis=0)
            if last is not None:
                h_ref[FINE * r : FINE * r + FINE, (k - 1) * 128 : k * 128] = jnp.where(cross, turned, last).astype(bf16)
            last = turned
    scale = 1.0 / math.sqrt(TIME)
    spot = [FINE * rr + FINE - 1 - lane % FINE for rr in range(4)]
    for j in range(2):
        begin = 128 - 128 * j
        summed = lax.dot_general(
            src_ref[:, begin : begin + DEPTH], h_ref[...], (((1,), (1,)), ((), ())), preferred_element_type=f32
        )
        summed = summed * scale
        for q in range(2):
            parts = [summed[64 * i : 64 * i + 64, 128 * q : 128 * q + 128] for i in range(4)]
            for rr in range(4):
                row = None
                for i in range(4):
                    moved = jnp.take_along_axis(parts[i], spot[rr], axis=1)
                    row = moved if row is None else jnp.where(lane // FINE == i, moved, row)
                for s in range(8):
                    out_ref[s, 4 * q + rr, :, 128 * j : 128 * j + 128] = row[8 * s : 8 * s + 8]


def correlate(place, own, other):
    return pl.pallas_call(
        corr_kernel,
        out_shape=jax.ShapeDtypeStruct((8, 8, 8, 256), jnp.float32),
        in_specs=[pl.BlockSpec(memory_space=pltpu.SMEM)] + [pl.BlockSpec(memory_space=pltpu.VMEM)] * 2,
        out_specs=pl.BlockSpec(memory_space=pltpu.VMEM),
        scratch_shapes=[
            pltpu.VMEM((8, LAG + TIME + 1280), jnp.float32),
            pltpu.VMEM((256, 128 + DEPTH), jnp.bfloat16),
            pltpu.VMEM((256, DEPTH), jnp.bfloat16),
        ],
        compiler_params=pltpu.CompilerParams(vmem_limit_bytes=24 << 20),
    )(place, own, other)


def on_device(traces, validity, owners):
    usable = traces * validity.astype(jnp.bfloat16)[:, None]
    halves = usable.reshape(8, 2, HALF).transpose(1, 0, 2)
    gathered = lax.all_to_all(jnp.tile(halves, (16, 1, 1)), CHAN, 0, 0)
    row = lax.axis_index(CHAN)[None]
    sent = pick(owners, row, gathered)
    own = lax.all_to_all(sent, TM, 0, 0)
    other = lax.ppermute(own, "core", [(0, 1), (1, 0)])
    place = jnp.stack([lax.axis_index("core"), lax.axis_index(TM)])
    return correlate(place, own, other)


def solution(mesh):
    fine = Mesh(mesh.devices.reshape(2, 8, 2, 2, 4), NAMES)
    return jax.shard_map(
        on_device,
        mesh=fine,
        in_specs=(P(CHAN, TM), P(CHAN), P()),
        out_specs=P(None, CHAN, None, TM),
        check_vma=False,
    )
```

time: 1210 us -> 49.6 us (0.04); the launches traced: 1200 us -> 49.3 us
  blocking collectives: 901 us -> 15.1 us
  local copies, waits for them, and re-layouts: 226 us -> 0.7 us
  other arithmetic: 35.6 us -> 1.51 us
  matrix products: 29.5 us -> 0 us
  starting transfers between devices: 0 us -> 14.3 us
    psum x8 -> x0, blocking collectives: 840 us -> none  [broadcast(): return lax.psum(block, axis)]
    reshape x12 -> x0, local copies, waits for them, and re-layouts: 123 us -> none  [toeplitz(): repeated.reshape(segment.shape[0], lag_rows, seg_width + 1)]
    while x60 -> x0, local copies, waits for them, and re-layouts: 86 us -> none
    all_gather x2 -> x0, blocking collectives: 60.8 us -> none  [the longest x1 32.3 us: on_device(): sources = lax.all_gather(source_pieces, 'tm', axis=2, tiled=True)]
    dot_general x12 -> x0, matrix products: 29.5 us -> none  [accumulate(): jnp.einsum('rku,scu->srck', shifted, source_block, preferred_element_type...]
    another operation x40 -> x1, other arithmetic: 27.6 us -> 0.07 us  [on_device(): place = jnp.stack([lax.axis_index('core'), lax.axis_index(TM)])]
    all_to_all x0 -> x1, blocking collectives: none -> 15.1 us  [on_device(): own = lax.all_to_all(sent, TM, 0, 0)]
  transfers between devices with their start and end apart: 0 -> 2, of which waited for: 0 -> 2; matrix products, arithmetic and copies ran while one was open for 0% -> 0% of each run, Pallas kernels for 0% -> 0%
where the time goes in v1:
time: 49.6 us; the launch traced here: 49.3 us
  blocking collectives  15.1 us (30%)
  starting transfers between devices  14.3 us (29%)
  waiting for transfers between devices  11.5 us (23%)
  Pallas kernels  6.09 us (12%)
  other arithmetic  1.51 us (3%)
  local copies, waits for them, and re-layouts  0.7 us (1%)
    all_to_all x1, blocking collectives, on_device(): own = lax.all_to_all(sent, TM, 0, 0)  15.1 us
    all_to_all x1, starting transfers between devices, on_device(): gathered = lax.all_to_all(jnp.tile(halves, (16, 1, 1)), CHAN, 0, 0)  11.1 us
    all_to_all x1, waiting for transfers between devices, on_device(): gathered = lax.all_to_all(jnp.tile(halves, (16, 1, 1)), CHAN, 0, 0)  10.1 us
    pallas_call x1, Pallas kernels, correlate(): pl.pallas_call(corr_kernel, out_shape=jax.ShapeDtypeStruct((8, 8, 8, 256)...  5.51 us
    ppermute x1, starting transfers between devices, on_device(): other = lax.ppermute(own, 'core', [(0, 1), (1, 0)])  3.22 us
    ppermute x1, waiting for transfers between devices, on_device(): other = lax.ppermute(own, 'core', [(0, 1), (1, 0)])  1.41 us
  transfers between devices with their start and end apart: 2, of which 2 were waited for; matrix products, arithmetic and copies ran while one was open for 0% of the time, Pallas kernels for 0%

profile of v1, /device:TPU:1, one launch (start us, length us, event | category | flops | bytes accessed | tf_op | source)
XLA Modules:
  0.0 49.3 jit_solution(12101404292425317513)
XLA Ops:
  0.0 0.7 %convert_element_type.3 = bf16[8]{0:T(256)(128)(2,1)S(1)} convert(s32[8]{0:T(128)} %param.4) | non-fusion elementwise | flops 8 | bytes 48 | tf_op jit(solution)/shard_map/convert_element_type | solution.py:111
  0.7 0.8 %broadcast_multiply_fusion = bf16[8,768]{1,0:T(8,128)(2,1)S(1)} fusion(bf16[8,768]{1,0:T(8,128)(2,1)} %param.3, bf16[8]{0:T(256)(128)(2,1)S(1)} %convert_element_type.3), kind=kLoop, calls=%fused_computation | loop fusion | flops 6144 | bytes 24592 | tf_op jit(solution)/shard_map/mul | solution.py:111
  1.4 0.7 %tile.4 = bf16[16,2,8,384]{3,2,1,0:T(8,128)(2,1)} broadcast(bf16[2,8,384]{2,1,0:T(8,128)(2,1)S(1)} %bitcast.7), dimensions={1,2,3} | broadcast | bytes 208896 | tf_op jit(solution)/shard_map/tile | solution.py:113
  2.1 11.1 %all-to-all-start = ((bf16[32,8,384]{2,1,0:T(8,128)(2,1)}), bf16[32,8,384]{2,1,0:T(8,128)(2,1)S(1)}, u32[]{:S(2)}, u32[]{:S(2)}) async-start(bf16[32,8,384]{2,1,0:T(8,128)(2,1)} %bitcast.5), calls=%async_computation | async-start | bytes 393216 | tf_op jit(solution)/shard_map/all_to_all | solution.py:113
  13.3 0.0 copy-start
  13.3 10.1 %all-to-all-done.gathered_ref = bf16[32,8,384]{2,1,0:T(8,128)(2,1)S(1)} async-done(((bf16[32,8,384]{2,1,0:T(8,128)(2,1)}), bf16[32,8,384]{2,1,0:T(8,128)(2,1)S(1)}, u32[]{:S(2)}, u32[]{:S(2)}) %all-to-all-start) | async-done | bytes 196640 | tf_op jit(solution)/shard_map/all_to_all | solution.py:113
  23.4 0.0 copy-done
  23.4 0.6 %shard_map.37 = bf16[8,80,384]{2,1,0:T(8,128)(2,1)S(1)} custom-call(s32[8]{0:T(128)S(1)} %copy-done, s32[1]{0:T(128)} %bitcast.2.row_ref, bf16[32,8,384]{2,1,0:T(8,128)(2,1)S(1)} %all-to-all-done.gathered_ref), custom_call_target="tpu_custom_call" | custom-call | tf_op jit(solution)/shard_map/pallas_call | solution.py:31
  24.0 15.1 %all_to_all.10.own_ref = bf16[8,80,384]{2,1,0:T(8,128)(2,1)S(1)} all-to-all(bf16[8,80,384]{2,1,0:T(8,128)(2,1)S(1)} %shard_map.37), channel_id=1, replica_groups=mesh['y_lo'=2,'z'=8,'core'=2,'y_hi'=2,'x'=4] {'y_hi','x'}, dimensions={0} | all-to-all | bytes 983040 | tf_op jit(solution)/shard_map/all_to_all | solution.py:116
  39.1 3.2 %collective-permute-start = (bf16[8,80,384]{2,1,0:T(8,128)(2,1)S(1)}, bf16[8,80,384]{2,1,0:T(8,128)(2,1)S(1)}, u32[]{:S(2)}, u32[]{:S(2)}) collective-permute-start(bf16[8,80,384]{2,1,0:T(8,128)(2,1)S(1)} %all_to_all.10.own_ref), channel_id=1, source_target_pairs={{0,8},{8,0},{1,9},{9,1},{2,10},{10,2},{3,11},{11,3},{4,12},{12,4},... | collective-permute-start | bytes 1474568 | tf_op jit(solution)/shard_map/ppermute | solution.py:117
  42.3 0.1 pad_add_fusion.place_ref
  42.4 1.4 %collective-permute-done.other_ref = bf16[8,80,384]{2,1,0:T(8,128)(2,1)S(1)} collective-permute-done((bf16[8,80,384]{2,1,0:T(8,128)(2,1)S(1)}, bf16[8,80,384]{2,1,0:T(8,128)(2,1)S(1)}, u32[]{:S(2)}, u32[]{:S(2)}) %collective-permute-start) | collective-permute-done | bytes 491552 | tf_op jit(solution)/shard_map/ppermute | solution.py:117
  43.8 5.5 %shard_map.38 = f32[8,8,8,256]{3,2,1,0:T(8,128)} custom-call(s32[2]{0:T(128)S(1)} %pad_add_fusion.place_ref, bf16[8,80,384]{2,1,0:T(8,128)(2,1)S(1)} %all_to_all.10.own_ref, bf16[8,80,384]{2,1,0:T(8,128)(2,1)S(1)} %collective-permute-done.other_ref), custom_call_target="tpu_custom_call" | custom-call | tf_op jit(solution)/shard_map/pallas_call | solution.py:96
Async XLA Ops:
  2.1 21.3 %all-to-all-start = ((bf16[32,8,384]{2,1,0:T(8,128)(2,1)}), bf16[32,8,384]{2,1,0:T(8,128)(2,1)S(1)}, u32[]{:S(2)}, u32[]{:S(2)}) async-start(bf16[32,8,384]{2,1,0:T(8,128)(2,1)} %bitcast.5), calls=%async_computation | async-start | bytes 393216 | tf_op jit(solution)/shard_map/all_to_all | solution.py:113
  13.3 10.1 %copy-start = (s32[8]{0:T(128)S(1)}, s32[8]{0:T(128)}, u32[]{:S(2)}) copy-start(s32[8]{0:T(128)} %owners_ref.1) | copy-start | bytes 100
  39.1 4.7 %collective-permute-start = (bf16[8,80,384]{2,1,0:T(8,128)(2,1)S(1)}, bf16[8,80,384]{2,1,0:T(8,128)(2,1)S(1)}, u32[]{:S(2)}, u32[]{:S(2)}) collective-permute-start(bf16[8,80,384]{2,1,0:T(8,128)(2,1)S(1)} %all_to_all.10.own_ref), channel_id=1, source_target_pairs={{0,8},{8,0},{1,9},{9,1},{2,10},{10,2},{3,11},{11,3},{4,12},{12,4},... | collective-permute-start | bytes 1474568 | tf_op jit(solution)/shard_map/ppermute | solution.py:117

commit v2 on v1

v2 whole, which is shorter than its diff:
```python
import math

import jax
import jax.numpy as jnp
from jax import lax
from jax.experimental import pallas as pl
from jax.experimental.pallas import tpu as pltpu
from jax.sharding import Mesh, PartitionSpec as P

LAG = 1024
TIME = 6144
PIECE = 768
FINE = 32
DEPTH = 6400
NAMES = ("y_lo", "z", "core", "y_hi", "x")
CHAN = ("y_lo", "z", "core")
TM = ("y_hi", "x")
CHAN_ORDER = list(range(31, -1, -1))
TM_ORDER = list(range(7, -1, -1))
CHAN_GROUPS = [[8 * c + m for c in CHAN_ORDER] for m in range(8)]
TM_GROUPS = [[8 * c + m for m in TM_ORDER] for c in range(32)]
f32, bf16 = jnp.float32, jnp.bfloat16
VMEM = pl.BlockSpec(memory_space=pltpu.VMEM)
SMALL = pltpu.CompilerParams(vmem_limit_bytes=4 << 20)


def prepare_kernel(traces_hbm, validity_hbm, owners_hbm, blocks_ref, mine_ref, owners_ref, traces_ref, validity_ref, sems):
    moves = [
        pltpu.make_async_copy(src, dst, sems.at[n])
        for n, (src, dst) in enumerate(
            ((traces_hbm, traces_ref), (validity_hbm, validity_ref), (owners_hbm, owners_ref))
        )
    ]
    for move in moves:
        move.start()
    for move in moves:
        move.wait()
    row = lax.broadcasted_iota(jnp.int32, (8, 8), 0)
    lane = lax.broadcasted_iota(jnp.int32, (8, 8), 1)
    flags = jnp.broadcast_to(validity_ref[...].astype(f32), (8, 8))
    flags = jnp.sum(jnp.where(row == lane, flags, 0.0), axis=1, keepdims=True)
    usable = (traces_ref[...].astype(f32) * flags).astype(bf16)
    mine_ref[...] = usable
    for place, device in enumerate(CHAN_ORDER):
        half = device % 2
        blocks_ref[place] = usable[4 * half : 4 * half + 4]


def prepare(traces, validity, owners):
    inputs = [pltpu.with_memory_space_constraint(v, pltpu.HBM) for v in (traces, validity.reshape(1, 8), owners.reshape(1, 8))]
    return pl.pallas_call(
        prepare_kernel,
        out_shape=(
            jax.ShapeDtypeStruct((32, 4, PIECE), bf16),
            jax.ShapeDtypeStruct((8, PIECE), bf16),
            jax.ShapeDtypeStruct((1, 8), jnp.int32),
        ),
        in_specs=[pl.BlockSpec(memory_space=pltpu.HBM)] * 3,
        out_specs=(VMEM, VMEM, VMEM),
        scratch_shapes=[pltpu.VMEM((8, PIECE), bf16), pltpu.VMEM((1, 8), jnp.int32), pltpu.SemaphoreType.DMA((3,))],
        compiler_params=SMALL,
    )(*inputs)


def pick_kernel(owners_ref, mine_ref, gathered_ref, out_ref):
    lane = lax.broadcasted_iota(jnp.int32, (1, 8), 1)
    owners = owners_ref[...]
    for peer in range(8):
        out_ref[peer, :8, :] = mine_ref[...]
    for s in range(8):
        block = gathered_ref[31 - jnp.sum(jnp.where(lane == s, owners, 0))]
        for peer in range(8):
            out_ref[peer, 8 + 4 * s : 12 + 4 * s, :] = block


def pick(owners, mine, gathered):
    return pl.pallas_call(
        pick_kernel,
        out_shape=jax.ShapeDtypeStruct((8, 40, PIECE), bf16),
        in_specs=[VMEM] * 3,
        out_specs=VMEM,
        compiler_params=SMALL,
    )(owners, mine, gathered)


def load_sources(pieces_ref, src_ref):
    src_ref[:, :256] = jnp.zeros((256, 256), bf16)
    src_ref[:, 128 + TIME :] = jnp.zeros((256, DEPTH - TIME), bf16)
    lane = lax.broadcasted_iota(jnp.int32, (32, 128), 1)
    before = [None] * 4
    for k in range(1, DEPTH // 128 + 1):
        t = 128 * (k - 1)
        if t < TIME:
            tile = pieces_ref[7 - t // PIECE, 8:40, t % PIECE : t % PIECE + 128]
        else:
            tile = jnp.zeros((32, 128), bf16)
        wide = tile.astype(f32)
        for i in range(4):
            if i == 0:
                value = tile
            else:
                turned = pltpu.roll(wide, FINE * i, 1)
                last = before[i] if before[i] is not None else jnp.zeros((32, 128), f32)
                value = jnp.where(lane < FINE * i, last, turned).astype(bf16)
                before[i] = turned
            src_ref[32 * i : 32 * i + 32, 128 * k : 128 * k + 128] = value
            if k < DEPTH // 128:
                src_ref[128 + 32 * i : 160 + 32 * i, 128 * k + 128 : 128 * k + 256] = value


def spread_receivers(pieces_ref, rec_ref, h_ref):
    rec_ref[:, :LAG] = jnp.zeros((8, LAG), f32)
    rec_ref[:, LAG + TIME :] = jnp.zeros((8, rec_ref.shape[1] - LAG - TIME), f32)
    for piece in range(8):
        at = LAG + PIECE * piece
        rec_ref[:, at : at + PIECE] = pieces_ref[7 - piece, :8, :].astype(f32)
    base = pl.multiple_of(256 * lax.axis_index(TM), 128)
    lane = lax.broadcasted_iota(jnp.int32, (FINE, 128), 1)
    row = lax.broadcasted_iota(jnp.int32, (FINE, 128), 0)
    cross = lane + (FINE - 1) - row >= 128
    for r in range(8):
        last = None
        for k in range(DEPTH // 128 + 1):
            wide = jnp.broadcast_to(rec_ref[r : r + 1, pl.ds(base + k * 128, 128)], (FINE, 128))
            turned = pltpu.roll(wide, 128 - (FINE - 1), 1, stride=1, stride_axis=0)
            if last is not None:
                h_ref[FINE * r : FINE * r + FINE, (k - 1) * 128 : k * 128] = jnp.where(cross, turned, last).astype(bf16)
            last = turned


def correlate(src_ref, h_ref, emit):
    summed = lax.dot_general(
        src_ref[:, 128 : 128 + DEPTH], h_ref[...], (((1,), (1,)), ((), ())), preferred_element_type=f32
    )
    summed = summed * (1.0 / math.sqrt(TIME))
    lane = lax.broadcasted_iota(jnp.int32, (32, 128), 1)
    spot = [FINE * q + FINE - 1 - lane % FINE for q in range(4)]
    for j in range(2):
        for half in range(2):
            for q in range(4):
                rows = None
                for i in range(4):
                    at = 128 * j + 32 * i
                    moved = jnp.take_along_axis(summed[at : at + 32, 128 * half : 128 * half + 128], spot[q], axis=1)
                    rows = moved if rows is None else jnp.where(lane // FINE == i, moved, rows)
                emit(j, 4 * half + q, rows)


def first_kernel(pieces_ref, h_ref, part_ref, rec_ref, src_ref):
    load_sources(pieces_ref, src_ref)
    spread_receivers(pieces_ref, rec_ref, h_ref)

    def emit(j, r, rows):
        part_ref[r, j] = rows

    correlate(src_ref, h_ref, emit)


def second_kernel(pieces_ref, h_ref, part_ref, out_ref, src_ref):
    load_sources(pieces_ref, src_ref)
    first = lax.axis_index("core") == 0
    low = lax.broadcasted_iota(jnp.int32, (8, 128), 0) < 4

    def emit(j, r, rows):
        mine = part_ref[r, j]
        for a in range(4):
            x, y = mine[8 * a : 8 * a + 8], rows[8 * a : 8 * a + 8]
            x, y = jnp.where(first, x, y), jnp.where(first, y, x)
            lags = slice(128 * j, 128 * j + 128)
            out_ref[2 * a, r, :, lags] = jnp.where(low, x, pltpu.roll(y, 4, 0))
            out_ref[2 * a + 1, r, :, lags] = jnp.where(low, pltpu.roll(x, 4, 0), y)

    correlate(src_ref, h_ref, emit)


COST = pl.CostEstimate(flops=2 * 256 * 256 * DEPTH, bytes_accessed=4 << 20, transcendentals=0)
LARGE = pltpu.CompilerParams(vmem_limit_bytes=16 << 20)
SOURCES = pltpu.VMEM((256, 128 + DEPTH), bf16)


def on_device(traces, validity, owners):
    blocks, mine, owners = prepare(traces, validity, owners)
    gathered = lax.all_to_all(blocks, NAMES, 0, 0, axis_index_groups=CHAN_GROUPS)
    own = lax.all_to_all(pick(owners, mine, gathered), NAMES, 0, 0, axis_index_groups=TM_GROUPS)
    other = lax.ppermute(own, "core", [(0, 1), (1, 0)])
    spread, part = pl.pallas_call(
        first_kernel,
        out_shape=(jax.ShapeDtypeStruct((256, DEPTH), bf16), jax.ShapeDtypeStruct((8, 2, 32, 128), f32)),
        in_specs=[VMEM],
        out_specs=(VMEM, VMEM),
        scratch_shapes=[pltpu.VMEM((8, LAG + TIME + 1280), f32), SOURCES],
        compiler_params=LARGE,
        cost_estimate=COST,
    )(own)
    return pl.pallas_call(
        second_kernel,
        out_shape=jax.ShapeDtypeStruct((8, 8, 8, 256), f32),
        in_specs=[VMEM] * 3,
        out_specs=VMEM,
        scratch_shapes=[SOURCES],
        compiler_params=LARGE,
        cost_estimate=COST,
    )(other, spread, part)


def solution(mesh):
    fine = Mesh(mesh.devices.reshape(2, 8, 2, 2, 4), NAMES)
    return jax.shard_map(
        on_device,
        mesh=fine,
        in_specs=(P(CHAN, TM), P(CHAN), P()),
        out_specs=P(None, CHAN, None, TM),
        check_vma=False,
    )
```

time: 49.6 us -> 40 us (0.81)
  blocking collectives: 15.1 us -> 33.5 us
  starting transfers between devices: 14.3 us -> 0.22 us
  waiting for transfers between devices: 11.5 us -> 0.01 us
  other arithmetic: 1.51 us -> 0 us
  local copies, waits for them, and re-layouts: 0.7 us -> 0 us
    all_to_all x1 -> x2, blocking collectives: 15.1 us -> 33.5 us  [the longest x1 18.9 us: on_device(): lax.all_to_all(blocks, NAMES, 0, 0, axis_index_groups=CHAN_GROUPS)]
    all_to_all x1 -> x0, starting transfers between devices: 11.1 us -> none  [on_device(): gathered = lax.all_to_all(jnp.tile(halves, (16, 1, 1)), CHAN, 0, 0)]
    all_to_all x1 -> x0, waiting for transfers between devices: 10.1 us -> none  [on_device(): gathered = lax.all_to_all(jnp.tile(halves, (16, 1, 1)), CHAN, 0, 0)]
    ppermute x1, starting transfers between devices: 3.22 us -> 0.22 us  [on_device(): other = lax.ppermute(own, 'core', [(0, 1), (1, 0)])]
    ppermute x1, waiting for transfers between devices: 1.41 us -> 0.01 us  [on_device(): other = lax.ppermute(own, 'core', [(0, 1), (1, 0)])]
    mul x1 -> x0, other arithmetic: 0.78 us -> none  [on_device(): usable = traces * validity.astype(jnp.bfloat16)[:, None]]
    another operation x1 -> x0, local copies, waits for them, and re-layouts: 0.7 us -> none  [on_device(): gathered = lax.all_to_all(jnp.tile(halves, (16, 1, 1)), CHAN, 0, 0)]
    convert_element_type x1 -> x0, other arithmetic: 0.66 us -> none  [on_device(): usable = traces * validity.astype(jnp.bfloat16)[:, None]]
  transfers between devices with their start and end apart: 2 -> 1, of which waited for: 2 -> 0; matrix products, arithmetic and copies ran while one was open for 0% -> 0% of each run, Pallas kernels for 0% -> 6%
where the time goes in v2:
time: 40 us; the launch traced here: 39.8 us
  blocking collectives  33.5 us (84%)
  Pallas kernels  6.12 us (15%)
    all_to_all x1, blocking collectives, on_device(): lax.all_to_all(blocks, NAMES, 0, 0, axis_index_groups=CHAN_GROUPS)  18.9 us
    all_to_all x1, blocking collectives, on_device(): lax.all_to_all(pick(owners, mine, gathered), NAMES, 0, 0, axis_index_grou...  14.5 us
    pallas_call x1, Pallas kernels, on_device(): pl.pallas_call(second_kernel, out_shape=jax.ShapeDtypeStruct((8, 8, 8, 25...  2.57 us
    pallas_call x1, Pallas kernels, on_device(): pl.pallas_call(first_kernel, out_shape=(jax.ShapeDtypeStruct((256, DEPTH)...  2.5 us
    pallas_call x1, Pallas kernels, prepare(): pl.pallas_call(prepare_kernel, out_shape=(jax.ShapeDtypeStruct((32, 4, PI...  0.83 us
  transfers between devices with their start and end apart: 1, of which 0 were waited for; matrix products, arithmetic and copies ran while one was open for 0% of the time, Pallas kernels for 6%

profile of v2, /device:TPU:1, one launch (start us, length us, event | category | flops | bytes accessed | tf_op | source)
XLA Modules:
  0.0 39.8 jit_solution(8623290176513109546)
XLA Ops:
  0.0 0.8 %shard_map.37 = (bf16[32,4,768]{2,1,0:T(4,128)(2,1)S(1)}, bf16[8,768]{1,0:T(8,128)(2,1)S(1)}, s32[1,8]{1,0:T(1,128)S(1)}) custom-call(bf16[8,768]{1,0:T(8,128)(2,1)} %traces_hbm.1, s32[1,8]{1,0:T(1,128)} %bitcast.2, s32[1,8]{1,0:T(1,128)} %bitcast.3), custom_call_target="tpu_custom_call" | custom-call | tf_op jit(solution)/shard_map/pallas_call | solution.py:51
  0.8 18.9 %all_to_all.10.gathered_ref = bf16[32,4,768]{2,1,0:T(4,128)(2,1)S(1)} all-to-all(bf16[32,4,768]{2,1,0:T(4,128)(2,1)S(1)} %get-tuple-element.12), channel_id=1, replica_groups={{248,240,232,224,216,208,200,192,184,176,168,160,152,144,136,128,120,11..., dimensions={0} | all-to-all | bytes 393216 | tf_op jit(solution)/shard_map/all_to_all | solution.py:183
  19.8 0.2 shard_map.38
  20.0 14.5 %all_to_all.11.pieces_ref = bf16[8,40,768]{2,1,0:T(8,128)(2,1)S(1)} all-to-all(bf16[8,40,768]{2,1,0:T(8,128)(2,1)S(1)} %shard_map.38), channel_id=1, replica_groups={{7,6,5,4,3,2,1,0},{15,14,13,12,11,10,9,8},{23,22,21,20,19,18,17,16},{31..., dimensions={0} | all-to-all | bytes 983040 | tf_op jit(solution)/shard_map/all_to_all | solution.py:184
  34.5 0.2 collective-permute-start
  34.7 2.5 %shard_map.39 = (bf16[256,6400]{1,0:T(8,128)(2,1)S(1)}, f32[8,2,32,128]{3,2,1,0:T(8,128)S(1)}) custom-call(bf16[8,40,768]{2,1,0:T(8,128)(2,1)S(1)} %all_to_all.11.pieces_ref), custom_call_target="tpu_custom_call" | custom-call | flops 838860800 | bytes 4194304 | tf_op jit(solution)/shard_map/pallas_call | solution.py:186
  37.2 0.0 collective-permute-done.pieces_ref
  37.3 2.6 %shard_map.40 = f32[8,8,8,256]{3,2,1,0:T(8,128)} custom-call(bf16[8,40,768]{2,1,0:T(8,128)(2,1)S(1)} %collective-permute-done.pieces_ref, bf16[256,6400]{1,0:T(8,128)(2,1)S(1)} %get-tuple-element.13.h_ref, f32[8,2,32,128]{3,2,1,0:T(8,128)S(1)} %get-tuple-element.14.part_ref), custom_call_target="tpu_custom_call" | custom-call | flops 838860800 | bytes 4194304 | tf_op jit(solution)/shard_map/pallas_call | solution.py:195
Async XLA Ops:
  34.5 2.7 %collective-permute-start = (bf16[8,40,768]{2,1,0:T(8,128)(2,1)S(1)}, bf16[8,40,768]{2,1,0:T(8,128)(2,1)S(1)}, u32[]{:S(2)}, u32[]{:S(2)}) collective-permute-start(bf16[8,40,768]{2,1,0:T(8,128)(2,1)S(1)} %all_to_all.11.pieces_ref), channel_id=1, source_target_pairs={{0,8},{8,0},{1,9},{9,1},{2,10},{10,2},{3,11},{11,3},{4,12},{12,4},... | collective-permute-start | bytes 1474568 | tf_op jit(solution)/shard_map/ppermute | solution.py:185

commit v3 on v2

--- a/solution.py
+++ b/solution.py
@@ -15,8 +15,9 @@
 NAMES = ("y_lo", "z", "core", "y_hi", "x")
 CHAN = ("y_lo", "z", "core")
 TM = ("y_hi", "x")
-CHAN_ORDER = list(range(31, -1, -1))
-TM_ORDER = list(range(7, -1, -1))
+CM, TMK = 27, 6
+CHAN_ORDER = [k ^ CM for k in range(32)]
+TM_ORDER = [k ^ TMK for k in range(8)]
 CHAN_GROUPS = [[8 * c + m for c in CHAN_ORDER] for m in range(8)]
 TM_GROUPS = [[8 * c + m for m in TM_ORDER] for c in range(32)]
 f32, bf16 = jnp.float32, jnp.bfloat16
@@ -68,7 +69,7 @@
     for peer in range(8):
         out_ref[peer, :8, :] = mine_ref[...]
     for s in range(8):
-        block = gathered_ref[31 - jnp.sum(jnp.where(lane == s, owners, 0))]
+        block = gathered_ref[jnp.bitwise_xor(jnp.sum(jnp.where(lane == s, owners, 0)), CM)]
         for peer in range(8):
             out_ref[peer, 8 + 4 * s : 12 + 4 * s, :] = block
 
@@ -83,15 +84,16 @@
     )(owners, mine, gathered)
 
 
-def load_sources(pieces_ref, src_ref):
+def start_sources(src_ref):
     src_ref[:, :256] = jnp.zeros((256, 256), bf16)
-    src_ref[:, 128 + TIME :] = jnp.zeros((256, DEPTH - TIME), bf16)
+
+
+def load_sources(pieces_ref, src_ref, begin, end, before):
     lane = lax.broadcasted_iota(jnp.int32, (32, 128), 1)
-    before = [None] * 4
-    for k in range(1, DEPTH // 128 + 1):
-        t = 128 * (k - 1)
+    for k in range(begin, end):
+        t = 128 * k
         if t < TIME:
-            tile = pieces_ref[7 - t // PIECE, 8:40, t % PIECE : t % PIECE + 128]
+            tile = pieces_ref[(t // PIECE) ^ TMK, 8:40, t % PIECE : t % PIECE + 128]
         else:
             tile = jnp.zeros((32, 128), bf16)
         wide = tile.astype(f32)
@@ -103,41 +105,56 @@
                 last = before[i] if before[i] is not None else jnp.zeros((32, 128), f32)
                 value = jnp.where(lane < FINE * i, last, turned).astype(bf16)
                 before[i] = turned
-            src_ref[32 * i : 32 * i + 32, 128 * k : 128 * k + 128] = value
-            if k < DEPTH // 128:
-                src_ref[128 + 32 * i : 160 + 32 * i, 128 * k + 128 : 128 * k + 256] = value
-
-
-def spread_receivers(pieces_ref, rec_ref, h_ref):
+            src_ref[32 * i : 32 * i + 32, 128 * k + 128 : 128 * k + 256] = value
+            if k + 1 < DEPTH // 128:
+                src_ref[128 + 32 * i : 160 + 32 * i, 128 * k + 256 : 128 * k + 384] = value
+
+
+def start_receivers(pieces_ref, rec_ref):
     rec_ref[:, :LAG] = jnp.zeros((8, LAG), f32)
     rec_ref[:, LAG + TIME :] = jnp.zeros((8, rec_ref.shape[1] - LAG - TIME), f32)
     for piece in range(8):
         at = LAG + PIECE * piece
-        rec_ref[:, at : at + PIECE] = pieces_ref[7 - piece, :8, :].astype(f32)
+        rec_ref[:, at : at + PIECE] = pieces_ref[piece ^ TMK, :8, :].astype(f32)
+
+
+def spread_receivers(rec_ref, h_ref, begin, end, before):
     base = pl.multiple_of(256 * lax.axis_index(TM), 128)
     lane = lax.broadcasted_iota(jnp.int32, (FINE, 128), 1)
     row = lax.broadcasted_iota(jnp.int32, (FINE, 128), 0)
     cross = lane + (FINE - 1) - row >= 128
     for r in range(8):
-        last = None
-        for k in range(DEPTH // 128 + 1):
+        for k in range(begin if begin == 0 else begin + 1, end + 1):
             wide = jnp.broadcast_to(rec_ref[r : r + 1, pl.ds(base + k * 128, 128)], (FINE, 128))
             turned = pltpu.roll(wide, 128 - (FINE - 1), 1, stride=1, stride_axis=0)
-            if last is not None:
-                h_ref[FINE * r : FINE * r + FINE, (k - 1) * 128 : k * 128] = jnp.where(cross, turned, last).astype(bf16)
-            last = turned
-
-
-def correlate(src_ref, h_ref, emit):
-    summed = lax.dot_general(
-        src_ref[:, 128 : 128 + DEPTH], h_ref[...], (((1,), (1,)), ((), ())), preferred_element_type=f32
-    )
+            if k > 0:
+                h_ref[FINE * r : FINE * r + FINE, (k - 1) * 128 : k * 128] = jnp.where(cross, turned, before[r]).astype(bf16)
+            before[r] = turned
+
+
+def multiply(src_ref, h_ref, chunks, prepare_chunk):
+    tiles = DEPTH // 128
+    summed = None
+    for n in range(chunks):
+        begin, end = tiles * n // chunks, tiles * (n + 1) // chunks
+        prepare_chunk(begin, end)
+        term = lax.dot_general(
+            src_ref[:, 128 + 128 * begin : 128 + 128 * end],
+            h_ref[:, 128 * begin : 128 * end],
+            (((1,), (1,)), ((), ())),
+            preferred_element_type=f32,
+        )
+        summed = term if summed is None else summed + term
+    return summed
+
+
+def arrange(summed, emit):
     summed = summed * (1.0 / math.sqrt(TIME))
     lane = lax.broadcasted_iota(jnp.int32, (32, 128), 1)
     spot = [FINE * q + FINE - 1 - lane % FINE for q in range(4)]
-    for j in range(2):
-        for half in range(2):
-            for q in range(4):
+    for half in range(2):
+        for q in range(4):
+            for j in range(2):
                 rows = None
                 for i in range(4):
                     at = 128 * j + 32 * i
@@ -147,19 +164,30 @@
 
 
 def first_kernel(pieces_ref, h_ref, part_ref, rec_ref, src_ref):
-    load_sources(pieces_ref, src_ref)
-    spread_receivers(pieces_ref, rec_ref, h_ref)
+    start_sources(src_ref)
+    start_receivers(pieces_ref, rec_ref)
+    sources, receivers = [None] * 4, [None] * 8
+
+    def chunk(begin, end):
+        load_sources(pieces_ref, src_ref, begin, end, sources)
+        spread_receivers(rec_ref, h_ref, begin, end, receivers)
 
     def emit(j, r, rows):
         part_ref[r, j] = rows
 
-    correlate(src_ref, h_ref, emit)
-
-
-def second_kernel(pieces_ref, h_ref, part_ref, out_ref, src_ref):
-    load_sources(pieces_ref, src_ref)
+    arrange(multiply(src_ref, h_ref, CHUNKS1, chunk), emit)
+
+
+def second_kernel(pieces_ref, h_ref, part_ref, out_hbm, src_ref, out_ref, sems):
+    start_sources(src_ref)
+    sources = [None] * 4
+
+    def chunk(begin, end):
+        load_sources(pieces_ref, src_ref, begin, end, sources)
+
     first = lax.axis_index("core") == 0
     low = lax.broadcasted_iota(jnp.int32, (8, 128), 0) < 4
+    moves = []
 
     def emit(j, r, rows):
         mine = part_ref[r, j]
@@ -167,12 +195,19 @@
             x, y = mine[8 * a : 8 * a + 8], rows[8 * a : 8 * a + 8]
             x, y = jnp.where(first, x, y), jnp.where(first, y, x)
             lags = slice(128 * j, 128 * j + 128)
-            out_ref[2 * a, r, :, lags] = jnp.where(low, x, pltpu.roll(y, 4, 0))
-            out_ref[2 * a + 1, r, :, lags] = jnp.where(low, pltpu.roll(x, 4, 0), y)
-
-    correlate(src_ref, h_ref, emit)
-
-
+            out_ref[r, 2 * a, :, lags] = jnp.where(low, x, pltpu.roll(y, 4, 0))
+            out_ref[r, 2 * a + 1, :, lags] = jnp.where(low, pltpu.roll(x, 4, 0), y)
+        if j == 1:
+            move = pltpu.make_async_copy(out_ref.at[r], out_hbm.at[:, r], sems.at[r])
+            move.start()
+            moves.append(move)
+
+    arrange(multiply(src_ref, h_ref, CHUNKS2, chunk), emit)
+    for move in moves:
+        move.wait()
+
+
+CHUNKS1, CHUNKS2 = 5, 5
 COST = pl.CostEstimate(flops=2 * 256 * 256 * DEPTH, bytes_accessed=4 << 20, transcendentals=0)
 LARGE = pltpu.CompilerParams(vmem_limit_bytes=16 << 20)
 SOURCES = pltpu.VMEM((256, 128 + DEPTH), bf16)
@@ -196,8 +231,8 @@
         second_kernel,
         out_shape=jax.ShapeDtypeStruct((8, 8, 8, 256), f32),
         in_specs=[VMEM] * 3,
-        out_specs=VMEM,
-        scratch_shapes=[SOURCES],
+        out_specs=pl.BlockSpec(memory_space=pltpu.HBM),
+        scratch_shapes=[SOURCES, pltpu.VMEM((8, 8, 8, 256), f32), pltpu.SemaphoreType.DMA((8,))],
         compiler_params=LARGE,
         cost_estimate=COST,
     )(other, spread, part)

time: 40 us -> 38.7 us (0.968)
  blocking collectives: 33.5 us -> 31.9 us
  starting transfers between devices: 0.22 us -> 0.71 us
    all_to_all x1, blocking collectives: 18.9 us -> 17.6 us  [on_device(): lax.all_to_all(blocks, NAMES, 0, 0, axis_index_groups=CHAN_GROUPS)]
    ppermute x1, starting transfers between devices: 0.22 us -> 0.71 us  [on_device(): other = lax.ppermute(own, 'core', [(0, 1), (1, 0)])]
where the time goes in v3:
time: 38.7 us; the launch traced here: 38.5 us
  blocking collectives  31.9 us (82%)
  Pallas kernels  5.78 us (15%)
  starting transfers between devices  0.71 us (2%)
    all_to_all x1, blocking collectives, on_device(): lax.all_to_all(blocks, NAMES, 0, 0, axis_index_groups=CHAN_GROUPS)  17.6 us
    all_to_all x1, blocking collectives, on_device(): lax.all_to_all(pick(owners, mine, gathered), NAMES, 0, 0, axis_index_grou...  14.3 us
    pallas_call x1, Pallas kernels, on_device(): pl.pallas_call(second_kernel, out_shape=jax.ShapeDtypeStruct((8, 8, 8, 25...  2.48 us
    pallas_call x1, Pallas kernels, on_device(): pl.pallas_call(first_kernel, out_shape=(jax.ShapeDtypeStruct((256, DEPTH)...  2.24 us
    pallas_call x1, Pallas kernels, prepare(): pl.pallas_call(prepare_kernel, out_shape=(jax.ShapeDtypeStruct((32, 4, PI...  0.83 us
  transfers between devices with their start and end apart: 1, of which 0 were waited for; matrix products, arithmetic and copies ran while one was open for 0% of the time, Pallas kernels for 6%

profile of v3, /device:TPU:1, one launch (start us, length us, event | category | flops | bytes accessed | tf_op | source)
XLA Modules:
  0.0 38.5 jit_solution(2028586625064741363)
XLA Ops:
  0.0 0.8 %shard_map.37 = (bf16[32,4,768]{2,1,0:T(4,128)(2,1)S(1)}, bf16[8,768]{1,0:T(8,128)(2,1)S(1)}, s32[1,8]{1,0:T(1,128)S(1)}) custom-call(bf16[8,768]{1,0:T(8,128)(2,1)} %traces_hbm.1, s32[1,8]{1,0:T(1,128)} %bitcast.2, s32[1,8]{1,0:T(1,128)} %bitcast.3), custom_call_target="tpu_custom_call" | custom-call | tf_op jit(solution)/shard_map/pallas_call | solution.py:52
  0.8 17.6 %all_to_all.10.gathered_ref = bf16[32,4,768]{2,1,0:T(4,128)(2,1)S(1)} all-to-all(bf16[32,4,768]{2,1,0:T(4,128)(2,1)S(1)} %get-tuple-element.12), channel_id=1, replica_groups={{216,208,200,192,248,240,232,224,152,144,136,128,184,176,168,160,88,80,..., dimensions={0} | all-to-all | bytes 393216 | tf_op jit(solution)/shard_map/all_to_all | solution.py:218
  18.4 0.2 shard_map.38
  18.7 14.3 %all_to_all.11.pieces_ref = bf16[8,40,768]{2,1,0:T(8,128)(2,1)S(1)} all-to-all(bf16[8,40,768]{2,1,0:T(8,128)(2,1)S(1)} %shard_map.38), channel_id=1, replica_groups={{6,7,4,5,2,3,0,1},{14,15,12,13,10,11,8,9},{22,23,20,21,18,19,16,17},{30..., dimensions={0} | all-to-all | bytes 983040 | tf_op jit(solution)/shard_map/all_to_all | solution.py:219
  33.0 0.7 %collective-permute-start = (bf16[8,40,768]{2,1,0:T(8,128)(2,1)S(1)}, bf16[8,40,768]{2,1,0:T(8,128)(2,1)S(1)}, u32[]{:S(2)}, u32[]{:S(2)}) collective-permute-start(bf16[8,40,768]{2,1,0:T(8,128)(2,1)S(1)} %all_to_all.11.pieces_ref), channel_id=1, source_target_pairs={{0,8},{8,0},{1,9},{9,1},{2,10},{10,2},{3,11},{11,3},{4,12},{12,4},... | collective-permute-start | bytes 1474568 | tf_op jit(solution)/shard_map/ppermute | solution.py:220
  33.7 2.2 %shard_map.39 = (bf16[256,6400]{1,0:T(8,128)(2,1)S(1)}, f32[8,2,32,128]{3,2,1,0:T(8,128)S(1)}) custom-call(bf16[8,40,768]{2,1,0:T(8,128)(2,1)S(1)} %all_to_all.11.pieces_ref), custom_call_target="tpu_custom_call" | custom-call | flops 838860800 | bytes 4194304 | tf_op jit(solution)/shard_map/pallas_call | solution.py:221
  36.0 0.0 collective-permute-done.pieces_ref
  36.0 2.5 %shard_map.40 = f32[8,8,8,256]{3,2,1,0:T(8,128)} custom-call(bf16[8,40,768]{2,1,0:T(8,128)(2,1)S(1)} %collective-permute-done.pieces_ref, bf16[256,6400]{1,0:T(8,128)(2,1)S(1)} %get-tuple-element.13.h_ref, f32[8,2,32,128]{3,2,1,0:T(8,128)S(1)} %get-tuple-element.14.part_ref), custom_call_target="tpu_custom_call" | custom-call | flops 838860800 | bytes 4194304 | tf_op jit(solution)/shard_map/pallas_call | solution.py:230
Async XLA Ops:
  33.0 3.0 %collective-permute-start = (bf16[8,40,768]{2,1,0:T(8,128)(2,1)S(1)}, bf16[8,40,768]{2,1,0:T(8,128)(2,1)S(1)}, u32[]{:S(2)}, u32[]{:S(2)}) collective-permute-start(bf16[8,40,768]{2,1,0:T(8,128)(2,1)S(1)} %all_to_all.11.pieces_ref), channel_id=1, source_target_pairs={{0,8},{8,0},{1,9},{9,1},{2,10},{10,2},{3,11},{11,3},{4,12},{12,4},... | collective-permute-start | bytes 1474568 | tf_op jit(solution)/shard_map/ppermute | solution.py:220

commit v4 on v3

--- a/solution.py
+++ b/solution.py
@@ -15,9 +15,23 @@
 NAMES = ("y_lo", "z", "core", "y_hi", "x")
 CHAN = ("y_lo", "z", "core")
 TM = ("y_hi", "x")
-CM, TMK = 27, 6
-CHAN_ORDER = [k ^ CM for k in range(32)]
-TM_ORDER = [k ^ TMK for k in range(8)]
+C_STRIDE, C_FIRST, C_STEP = (1, 2, 16), (1, 5, 1), 1
+T_STRIDE, T_FIRST, T_STEP = (4, 1), (1, 2), 1
+
+
+def chan_place(device):
+    lo, z, core = device // 16, device // 2 % 8, device % 2
+    place = C_STRIDE[0] * ((lo + C_FIRST[0]) % 2) + C_STRIDE[2] * ((core + C_FIRST[2]) % 2)
+    return place + C_STRIDE[1] * ((C_STEP * (z + 8 - C_FIRST[1])) % 8)
+
+
+def tm_place(device):
+    hi, x = device // 4, device % 4
+    return T_STRIDE[0] * ((hi + T_FIRST[0]) % 2) + T_STRIDE[1] * ((T_STEP * (x + 4 - T_FIRST[1])) % 4)
+
+
+CHAN_ORDER = sorted(range(32), key=chan_place)
+TM_ORDER = sorted(range(8), key=tm_place)
 CHAN_GROUPS = [[8 * c + m for c in CHAN_ORDER] for m in range(8)]
 TM_GROUPS = [[8 * c + m for m in TM_ORDER] for c in range(32)]
 f32, bf16 = jnp.float32, jnp.bfloat16
@@ -69,7 +83,7 @@
     for peer in range(8):
         out_ref[peer, :8, :] = mine_ref[...]
     for s in range(8):
-        block = gathered_ref[jnp.bitwise_xor(jnp.sum(jnp.where(lane == s, owners, 0)), CM)]
+        block = gathered_ref[chan_place(jnp.sum(jnp.where(lane == s, owners, 0)))]
         for peer in range(8):
             out_ref[peer, 8 + 4 * s : 12 + 4 * s, :] = block
 
@@ -85,7 +99,7 @@
 
 
 def start_sources(src_ref):
-    src_ref[:, :256] = jnp.zeros((256, 256), bf16)
+    src_ref[:, :128] = jnp.zeros((128, 128), bf16)
 
 
 def load_sources(pieces_ref, src_ref, begin, end, before):
@@ -93,7 +107,7 @@
     for k in range(begin, end):
         t = 128 * k
         if t < TIME:
-            tile = pieces_ref[(t // PIECE) ^ TMK, 8:40, t % PIECE : t % PIECE + 128]
+            tile = pieces_ref[tm_place(t // PIECE), 8:40, t % PIECE : t % PIECE + 128]
         else:
             tile = jnp.zeros((32, 128), bf16)
         wide = tile.astype(f32)
@@ -106,8 +120,6 @@
                 value = jnp.where(lane < FINE * i, last, turned).astype(bf16)
                 before[i] = turned
             src_ref[32 * i : 32 * i + 32, 128 * k + 128 : 128 * k + 256] = value
-            if k + 1 < DEPTH // 128:
-                src_ref[128 + 32 * i : 160 + 32 * i, 128 * k + 256 : 128 * k + 384] = value
 
 
 def start_receivers(pieces_ref, rec_ref):
@@ -115,7 +127,7 @@
     rec_ref[:, LAG + TIME :] = jnp.zeros((8, rec_ref.shape[1] - LAG - TIME), f32)
     for piece in range(8):
         at = LAG + PIECE * piece
-        rec_ref[:, at : at + PIECE] = pieces_ref[piece ^ TMK, :8, :].astype(f32)
+        rec_ref[:, at : at + PIECE] = pieces_ref[tm_place(piece), :8, :].astype(f32)
 
 
 def spread_receivers(rec_ref, h_ref, begin, end, before):
@@ -138,8 +150,9 @@
     for n in range(chunks):
         begin, end = tiles * n // chunks, tiles * (n + 1) // chunks
         prepare_chunk(begin, end)
+        shifted = [src_ref[:, 128 * (begin + 1 - j) : 128 * (end + 1 - j)] for j in range(2)]
         term = lax.dot_general(
-            src_ref[:, 128 + 128 * begin : 128 + 128 * end],
+            jnp.concatenate(shifted, axis=0),
             h_ref[:, 128 * begin : 128 * end],
             (((1,), (1,)), ((), ())),
             preferred_element_type=f32,
@@ -151,16 +164,17 @@
 def arrange(summed, emit):
     summed = summed * (1.0 / math.sqrt(TIME))
     lane = lax.broadcasted_iota(jnp.int32, (32, 128), 1)
-    spot = [FINE * q + FINE - 1 - lane % FINE for q in range(4)]
+    group = lane // FINE
+    spot = [(group + q) % 4 * FINE + FINE - 1 - lane % FINE for q in range(4)]
     for half in range(2):
+        turned = [[summed[128 * j + 32 * i : 128 * j + 32 * i + 32, 128 * half : 128 * half + 128] for i in range(4)] for j in range(2)]
+        turned = [[t[0]] + [pltpu.roll(t[i], FINE * i, 1) for i in range(1, 4)] for t in turned]
         for q in range(4):
             for j in range(2):
-                rows = None
-                for i in range(4):
-                    at = 128 * j + 32 * i
-                    moved = jnp.take_along_axis(summed[at : at + 32, 128 * half : 128 * half + 128], spot[q], axis=1)
-                    rows = moved if rows is None else jnp.where(lane // FINE == i, moved, rows)
-                emit(j, 4 * half + q, rows)
+                rows = turned[j][0]
+                for i in range(1, 4):
+                    rows = jnp.where(group == (q + i) % 4, turned[j][i], rows)
+                emit(j, 4 * half + q, jnp.take_along_axis(rows, spot[q], axis=1))
 
 
 def first_kernel(pieces_ref, h_ref, part_ref, rec_ref, src_ref):
@@ -210,7 +224,7 @@
 CHUNKS1, CHUNKS2 = 5, 5
 COST = pl.CostEstimate(flops=2 * 256 * 256 * DEPTH, bytes_accessed=4 << 20, transcendentals=0)
 LARGE = pltpu.CompilerParams(vmem_limit_bytes=16 << 20)
-SOURCES = pltpu.VMEM((256, 128 + DEPTH), bf16)
+SOURCES = pltpu.VMEM((128, 128 + DEPTH), bf16)
 
 
 def on_device(traces, validity, owners):

time: 38.7 us -> 38.2 us (0.987)
  no operation moved by 1% of the time
where the time goes in v4:
time: 38.2 us; the launch traced here: 38 us
  blocking collectives  31.6 us (83%)
  Pallas kernels  5.52 us (14%)
  starting transfers between devices  0.85 us (2%)
    all_to_all x1, blocking collectives, on_device(): lax.all_to_all(blocks, NAMES, 0, 0, axis_index_groups=CHAN_GROUPS)  17.3 us
    all_to_all x1, blocking collectives, on_device(): lax.all_to_all(pick(owners, mine, gathered), NAMES, 0, 0, axis_index_grou...  14.2 us
    pallas_call x1, Pallas kernels, on_device(): pl.pallas_call(second_kernel, out_shape=jax.ShapeDtypeStruct((8, 8, 8, 25...  2.19 us
    pallas_call x1, Pallas kernels, on_device(): pl.pallas_call(first_kernel, out_shape=(jax.ShapeDtypeStruct((256, DEPTH)...  2.18 us
    ppermute x1, starting transfers between devices, on_device(): other = lax.ppermute(own, 'core', [(0, 1), (1, 0)])  0.85 us
    pallas_call x1, Pallas kernels, prepare(): pl.pallas_call(prepare_kernel, out_shape=(jax.ShapeDtypeStruct((32, 4, PI...  0.83 us
  transfers between devices with their start and end apart: 1, of which 0 were waited for; matrix products, arithmetic and copies ran while one was open for 0% of the time, Pallas kernels for 6%

profile of v4, /device:TPU:1, one launch (start us, length us, event | category | flops | bytes accessed | tf_op | source)
XLA Modules:
  0.0 38.0 jit_solution(3928529841917463134)
XLA Ops:
  0.0 0.8 %shard_map.37 = (bf16[32,4,768]{2,1,0:T(4,128)(2,1)S(1)}, bf16[8,768]{1,0:T(8,128)(2,1)S(1)}, s32[1,8]{1,0:T(1,128)S(1)}) custom-call(bf16[8,768]{1,0:T(8,128)(2,1)} %traces_hbm.1, s32[1,8]{1,0:T(1,128)} %bitcast.2, s32[1,8]{1,0:T(1,128)} %bitcast.3), custom_call_target="tpu_custom_call" | custom-call | tf_op jit(solution)/shard_map/pallas_call | solution.py:66
  0.8 17.3 %all_to_all.10.gathered_ref = bf16[32,4,768]{2,1,0:T(4,128)(2,1)S(1)} all-to-all(bf16[32,4,768]{2,1,0:T(4,128)(2,1)S(1)} %get-tuple-element.12), channel_id=1, replica_groups={{216,88,232,104,248,120,136,8,152,24,168,40,184,56,200,72,208,80,224,96..., dimensions={0} | all-to-all | bytes 393216 | tf_op jit(solution)/shard_map/all_to_all | solution.py:232
  18.2 0.3 shard_map.38
  18.5 14.2 %all_to_all.11.pieces_ref = bf16[8,40,768]{2,1,0:T(8,128)(2,1)S(1)} all-to-all(bf16[8,40,768]{2,1,0:T(8,128)(2,1)S(1)} %shard_map.38), channel_id=1, replica_groups={{6,7,4,5,2,3,0,1},{14,15,12,13,10,11,8,9},{22,23,20,21,18,19,16,17},{30..., dimensions={0} | all-to-all | bytes 983040 | tf_op jit(solution)/shard_map/all_to_all | solution.py:233
  32.7 0.9 %collective-permute-start = (bf16[8,40,768]{2,1,0:T(8,128)(2,1)S(1)}, bf16[8,40,768]{2,1,0:T(8,128)(2,1)S(1)}, u32[]{:S(2)}, u32[]{:S(2)}) collective-permute-start(bf16[8,40,768]{2,1,0:T(8,128)(2,1)S(1)} %all_to_all.11.pieces_ref), channel_id=1, source_target_pairs={{0,8},{8,0},{1,9},{9,1},{2,10},{10,2},{3,11},{11,3},{4,12},{12,4},... | collective-permute-start | bytes 1474568 | tf_op jit(solution)/shard_map/ppermute | solution.py:234
  33.6 2.2 %shard_map.39 = (bf16[256,6400]{1,0:T(8,128)(2,1)S(1)}, f32[8,2,32,128]{3,2,1,0:T(8,128)S(1)}) custom-call(bf16[8,40,768]{2,1,0:T(8,128)(2,1)S(1)} %all_to_all.11.pieces_ref), custom_call_target="tpu_custom_call" | custom-call | flops 838860800 | bytes 4194304 | tf_op jit(solution)/shard_map/pallas_call | solution.py:235
  35.8 0.0 collective-permute-done.pieces_ref
  35.8 2.2 %shard_map.40 = f32[8,8,8,256]{3,2,1,0:T(8,128)} custom-call(bf16[8,40,768]{2,1,0:T(8,128)(2,1)S(1)} %collective-permute-done.pieces_ref, bf16[256,6400]{1,0:T(8,128)(2,1)S(1)} %get-tuple-element.13.h_ref, f32[8,2,32,128]{3,2,1,0:T(8,128)S(1)} %get-tuple-element.14.part_ref), custom_call_target="tpu_custom_call" | custom-call | flops 838860800 | bytes 4194304 | tf_op jit(solution)/shard_map/pallas_call | solution.py:244
Async XLA Ops:
  32.7 3.0 %collective-permute-start = (bf16[8,40,768]{2,1,0:T(8,128)(2,1)S(1)}, bf16[8,40,768]{2,1,0:T(8,128)(2,1)S(1)}, u32[]{:S(2)}, u32[]{:S(2)}) collective-permute-start(bf16[8,40,768]{2,1,0:T(8,128)(2,1)S(1)} %all_to_all.11.pieces_ref), channel_id=1, source_target_pairs={{0,8},{8,0},{1,9},{9,1},{2,10},{10,2},{3,11},{11,3},{4,12},{12,4},... | collective-permute-start | bytes 1474568 | tf_op jit(solution)/shard_map/ppermute | solution.py:234

commit v5 on v4

--- a/solution.py
+++ b/solution.py
@@ -16,7 +16,7 @@
 CHAN = ("y_lo", "z", "core")
 TM = ("y_hi", "x")
 C_STRIDE, C_FIRST, C_STEP = (1, 2, 16), (1, 5, 1), 1
-T_STRIDE, T_FIRST, T_STEP = (4, 1), (1, 2), 1
+T_STRIDE, T_FIRST, T_STEP = ((4, 1), (1, 2)), ((1, 2), (1, 2)), (1, 1)
 
 
 def chan_place(device):
@@ -25,15 +25,20 @@
     return place + C_STRIDE[1] * ((C_STEP * (z + 8 - C_FIRST[1])) % 8)
 
 
-def tm_place(device):
+def tm_place(device, core):
     hi, x = device // 4, device % 4
-    return T_STRIDE[0] * ((hi + T_FIRST[0]) % 2) + T_STRIDE[1] * ((T_STEP * (x + 4 - T_FIRST[1])) % 4)
+    place = T_STRIDE[core][0] * ((hi + T_FIRST[core][0]) % 2)
+    return place + T_STRIDE[core][1] * ((T_STEP[core] * (x + 4 - T_FIRST[core][1])) % 4)
+
+
+def tm_places(core):
+    return [jnp.where(core == 0, tm_place(m, 0), tm_place(m, 1)) for m in range(8)]
 
 
 CHAN_ORDER = sorted(range(32), key=chan_place)
-TM_ORDER = sorted(range(8), key=tm_place)
+TM_ORDER = [sorted(range(8), key=lambda m: tm_place(m, core)) for core in range(2)]
 CHAN_GROUPS = [[8 * c + m for c in CHAN_ORDER] for m in range(8)]
-TM_GROUPS = [[8 * c + m for m in TM_ORDER] for c in range(32)]
+TM_GROUPS = [[8 * c + m for m in TM_ORDER[c % 2]] for c in range(32)]
 f32, bf16 = jnp.float32, jnp.bfloat16
 VMEM = pl.BlockSpec(memory_space=pltpu.VMEM)
 SMALL = pltpu.CompilerParams(vmem_limit_bytes=4 << 20)
@@ -79,11 +84,11 @@
 
 def pick_kernel(owners_ref, mine_ref, gathered_ref, out_ref):
     lane = lax.broadcasted_iota(jnp.int32, (1, 8), 1)
-    owners = owners_ref[...]
+    places = chan_place(owners_ref[...])
     for peer in range(8):
         out_ref[peer, :8, :] = mine_ref[...]
     for s in range(8):
-        block = gathered_ref[chan_place(jnp.sum(jnp.where(lane == s, owners, 0)))]
+        block = gathered_ref[jnp.sum(jnp.where(lane == s, places, 0))]
         for peer in range(8):
             out_ref[peer, 8 + 4 * s : 12 + 4 * s, :] = block
 
@@ -102,12 +107,12 @@
     src_ref[:, :128] = jnp.zeros((128, 128), bf16)
 
 
-def load_sources(pieces_ref, src_ref, begin, end, before):
+def load_sources(pieces_ref, places, src_ref, begin, end, before):
     lane = lax.broadcasted_iota(jnp.int32, (32, 128), 1)
     for k in range(begin, end):
         t = 128 * k
         if t < TIME:
-            tile = pieces_ref[tm_place(t // PIECE), 8:40, t % PIECE : t % PIECE + 128]
+            tile = pieces_ref[places[t // PIECE], 8:40, t % PIECE : t % PIECE + 128]
         else:
             tile = jnp.zeros((32, 128), bf16)
         wide = tile.astype(f32)
@@ -122,12 +127,12 @@
             src_ref[32 * i : 32 * i + 32, 128 * k + 128 : 128 * k + 256] = value
 
 
-def start_receivers(pieces_ref, rec_ref):
+def start_receivers(pieces_ref, places, rec_ref):
     rec_ref[:, :LAG] = jnp.zeros((8, LAG), f32)
     rec_ref[:, LAG + TIME :] = jnp.zeros((8, rec_ref.shape[1] - LAG - TIME), f32)
     for piece in range(8):
         at = LAG + PIECE * piece
-        rec_ref[:, at : at + PIECE] = pieces_ref[tm_place(piece), :8, :].astype(f32)
+        rec_ref[:, at : at + PIECE] = pieces_ref[places[piece], :8, :].astype(f32)
 
 
 def spread_receivers(rec_ref, h_ref, begin, end, before):
@@ -138,9 +143,9 @@
     for r in range(8):
         for k in range(begin if begin == 0 else begin + 1, end + 1):
             wide = jnp.broadcast_to(rec_ref[r : r + 1, pl.ds(base + k * 128, 128)], (FINE, 128))
-            turned = pltpu.roll(wide, 128 - (FINE - 1), 1, stride=1, stride_axis=0)
+            turned = pltpu.roll(wide, 128 - (FINE - 1), 1, stride=1, stride_axis=0).astype(bf16)
             if k > 0:
-                h_ref[FINE * r : FINE * r + FINE, (k - 1) * 128 : k * 128] = jnp.where(cross, turned, before[r]).astype(bf16)
+                h_ref[FINE * r : FINE * r + FINE, (k - 1) * 128 : k * 128] = jnp.where(cross, turned, before[r])
             before[r] = turned
 
 
@@ -178,12 +183,13 @@
 
 
 def first_kernel(pieces_ref, h_ref, part_ref, rec_ref, src_ref):
+    places = tm_places(lax.axis_index("core"))
     start_sources(src_ref)
-    start_receivers(pieces_ref, rec_ref)
+    start_receivers(pieces_ref, places, rec_ref)
     sources, receivers = [None] * 4, [None] * 8
 
     def chunk(begin, end):
-        load_sources(pieces_ref, src_ref, begin, end, sources)
+        load_sources(pieces_ref, places, src_ref, begin, end, sources)
         spread_receivers(rec_ref, h_ref, begin, end, receivers)
 
     def emit(j, r, rows):
@@ -193,11 +199,12 @@
 
 
 def second_kernel(pieces_ref, h_ref, part_ref, out_hbm, src_ref, out_ref, sems):
+    places = tm_places(1 - lax.axis_index("core"))
     start_sources(src_ref)
     sources = [None] * 4
 
     def chunk(begin, end):
-        load_sources(pieces_ref, src_ref, begin, end, sources)
+        load_sources(pieces_ref, places, src_ref, begin, end, sources)
 
     first = lax.axis_index("core") == 0
     low = lax.broadcasted_iota(jnp.int32, (8, 128), 0) < 4

time: 38.2 us -> 38.1 us (level)
  blocking collectives: 31.6 us -> 31.1 us
  starting transfers between devices: 0.85 us -> 1.26 us
    all_to_all x1, blocking collectives: 14.2 us -> 13.8 us  [on_device(): lax.all_to_all(pick(owners, mine, gathered), NAMES, 0, 0, axis_index_grou...]
    ppermute x1, starting transfers between devices: 0.85 us -> 1.26 us  [on_device(): other = lax.ppermute(own, 'core', [(0, 1), (1, 0)])]
where the time goes in v5:
time: 38.1 us; the launch traced here: 37.9 us
  blocking collectives  31.1 us (82%)
  Pallas kernels  5.45 us (14%)
  starting transfers between devices  1.26 us (3%)
    all_to_all x1, blocking collectives, on_device(): lax.all_to_all(blocks, NAMES, 0, 0, axis_index_groups=CHAN_GROUPS)  17.3 us
    all_to_all x1, blocking collectives, on_device(): lax.all_to_all(pick(owners, mine, gathered), NAMES, 0, 0, axis_index_grou...  13.8 us
    pallas_call x1, Pallas kernels, on_device(): pl.pallas_call(second_kernel, out_shape=jax.ShapeDtypeStruct((8, 8, 8, 25...  2.21 us
    pallas_call x1, Pallas kernels, on_device(): pl.pallas_call(first_kernel, out_shape=(jax.ShapeDtypeStruct((256, DEPTH)...  2.16 us
    ppermute x1, starting transfers between devices, on_device(): other = lax.ppermute(own, 'core', [(0, 1), (1, 0)])  1.26 us
    pallas_call x1, Pallas kernels, prepare(): pl.pallas_call(prepare_kernel, out_shape=(jax.ShapeDtypeStruct((32, 4, PI...  0.83 us
  transfers between devices with their start and end apart: 1, of which 0 were waited for; matrix products, arithmetic and copies ran while one was open for 0% of the time, Pallas kernels for 6%

profile of v5, /device:TPU:1, one launch (start us, length us, event | category | flops | bytes accessed | tf_op | source)
XLA Modules:
  0.0 37.9 jit_solution(8017399870103511236)
XLA Ops:
  0.0 0.8 %shard_map.37 = (bf16[32,4,768]{2,1,0:T(4,128)(2,1)S(1)}, bf16[8,768]{1,0:T(8,128)(2,1)S(1)}, s32[1,8]{1,0:T(1,128)S(1)}) custom-call(bf16[8,768]{1,0:T(8,128)(2,1)} %traces_hbm.1, s32[1,8]{1,0:T(1,128)} %bitcast.2, s32[1,8]{1,0:T(1,128)} %bitcast.3), custom_call_target="tpu_custom_call" | custom-call | tf_op jit(solution)/shard_map/pallas_call | solution.py:71
  0.8 17.3 %all_to_all.10.gathered_ref = bf16[32,4,768]{2,1,0:T(4,128)(2,1)S(1)} all-to-all(bf16[32,4,768]{2,1,0:T(4,128)(2,1)S(1)} %get-tuple-element.12), channel_id=1, replica_groups={{216,88,232,104,248,120,136,8,152,24,168,40,184,56,200,72,208,80,224,96..., dimensions={0} | all-to-all | bytes 393216 | tf_op jit(solution)/shard_map/all_to_all | solution.py:239
  18.2 0.2 shard_map.38
  18.4 13.8 %all_to_all.11.pieces_ref = bf16[8,40,768]{2,1,0:T(8,128)(2,1)S(1)} all-to-all(bf16[8,40,768]{2,1,0:T(8,128)(2,1)S(1)} %shard_map.38), channel_id=1, replica_groups={{6,7,4,5,2,3,0,1},{14,10,15,11,12,8,13,9},{22,23,20,21,18,19,16,17},{30..., dimensions={0} | all-to-all | bytes 983040 | tf_op jit(solution)/shard_map/all_to_all | solution.py:240
  32.2 1.3 %collective-permute-start = (bf16[8,40,768]{2,1,0:T(8,128)(2,1)S(1)}, bf16[8,40,768]{2,1,0:T(8,128)(2,1)S(1)}, u32[]{:S(2)}, u32[]{:S(2)}) collective-permute-start(bf16[8,40,768]{2,1,0:T(8,128)(2,1)S(1)} %all_to_all.11.pieces_ref), channel_id=1, source_target_pairs={{0,8},{8,0},{1,9},{9,1},{2,10},{10,2},{3,11},{11,3},{4,12},{12,4},... | collective-permute-start | bytes 1474568 | tf_op jit(solution)/shard_map/ppermute | solution.py:241
  33.5 2.2 %shard_map.39 = (bf16[256,6400]{1,0:T(8,128)(2,1)S(1)}, f32[8,2,32,128]{3,2,1,0:T(8,128)S(1)}) custom-call(bf16[8,40,768]{2,1,0:T(8,128)(2,1)S(1)} %all_to_all.11.pieces_ref), custom_call_target="tpu_custom_call" | custom-call | flops 838860800 | bytes 4194304 | tf_op jit(solution)/shard_map/pallas_call | solution.py:242
  35.7 0.0 collective-permute-done.pieces_ref
  35.7 2.2 %shard_map.40 = f32[8,8,8,256]{3,2,1,0:T(8,128)} custom-call(bf16[8,40,768]{2,1,0:T(8,128)(2,1)S(1)} %collective-permute-done.pieces_ref, bf16[256,6400]{1,0:T(8,128)(2,1)S(1)} %get-tuple-element.13.h_ref, f32[8,2,32,128]{3,2,1,0:T(8,128)S(1)} %get-tuple-element.14.part_ref), custom_call_target="tpu_custom_call" | custom-call | flops 838860800 | bytes 4194304 | tf_op jit(solution)/shard_map/pallas_call | solution.py:251
Async XLA Ops:
  32.2 3.4 %collective-permute-start = (bf16[8,40,768]{2,1,0:T(8,128)(2,1)S(1)}, bf16[8,40,768]{2,1,0:T(8,128)(2,1)S(1)}, u32[]{:S(2)}, u32[]{:S(2)}) collective-permute-start(bf16[8,40,768]{2,1,0:T(8,128)(2,1)S(1)} %all_to_all.11.pieces_ref), channel_id=1, source_target_pairs={{0,8},{8,0},{1,9},{9,1},{2,10},{10,2},{3,11},{11,3},{4,12},{12,4},... | collective-permute-start | bytes 1474568 | tf_op jit(solution)/shard_map/ppermute | solution.py:241

commit v6 on v5

--- a/solution.py
+++ b/solution.py
@@ -150,10 +150,9 @@
 
 
 def multiply(src_ref, h_ref, chunks, prepare_chunk):
-    tiles = DEPTH // 128
     summed = None
-    for n in range(chunks):
-        begin, end = tiles * n // chunks, tiles * (n + 1) // chunks
+    for n in range(len(chunks) - 1):
+        begin, end = chunks[n], chunks[n + 1]
         prepare_chunk(begin, end)
         shifted = [src_ref[:, 128 * (begin + 1 - j) : 128 * (end + 1 - j)] for j in range(2)]
         term = lax.dot_general(
@@ -228,7 +227,7 @@
         move.wait()
 
 
-CHUNKS1, CHUNKS2 = 5, 5
+CHUNKS1, CHUNKS2 = (0, 4, 14, 24, 34, 44, 50), (0, 2, 6, 50)
 COST = pl.CostEstimate(flops=2 * 256 * 256 * DEPTH, bytes_accessed=4 << 20, transcendentals=0)
 LARGE = pltpu.CompilerParams(vmem_limit_bytes=16 << 20)
 SOURCES = pltpu.VMEM((128, 128 + DEPTH), bf16)

time: 38.1 us -> 38.1 us (level)
  no operation moved by 1% of the time
where the time goes in v6:
time: 38.1 us; the launch traced here: 37.9 us
  blocking collectives  31.1 us (82%)
  Pallas kernels  5.49 us (14%)
  starting transfers between devices  1.26 us (3%)
    all_to_all x1, blocking collectives, on_device(): lax.all_to_all(blocks, NAMES, 0, 0, axis_index_groups=CHAN_GROUPS)  17.3 us
    all_to_all x1, blocking collectives, on_device(): lax.all_to_all(pick(owners, mine, gathered), NAMES, 0, 0, axis_index_grou...  13.8 us
    pallas_call x1, Pallas kernels, on_device(): pl.pallas_call(second_kernel, out_shape=jax.ShapeDtypeStruct((8, 8, 8, 25...  2.22 us
    pallas_call x1, Pallas kernels, on_device(): pl.pallas_call(first_kernel, out_shape=(jax.ShapeDtypeStruct((256, DEPTH)...  2.2 us
    ppermute x1, starting transfers between devices, on_device(): other = lax.ppermute(own, 'core', [(0, 1), (1, 0)])  1.26 us
    pallas_call x1, Pallas kernels, prepare(): pl.pallas_call(prepare_kernel, out_shape=(jax.ShapeDtypeStruct((32, 4, PI...  0.83 us
  transfers between devices with their start and end apart: 1, of which 0 were waited for; matrix products, arithmetic and copies ran while one was open for 0% of the time, Pallas kernels for 6%

profile of v6, /device:TPU:1, one launch (start us, length us, event | category | flops | bytes accessed | tf_op | source)
XLA Modules:
  0.0 37.9 jit_solution(17490578269711120272)
XLA Ops:
  0.0 0.8 %shard_map.37 = (bf16[32,4,768]{2,1,0:T(4,128)(2,1)S(1)}, bf16[8,768]{1,0:T(8,128)(2,1)S(1)}, s32[1,8]{1,0:T(1,128)S(1)}) custom-call(bf16[8,768]{1,0:T(8,128)(2,1)} %traces_hbm.1, s32[1,8]{1,0:T(1,128)} %bitcast.2, s32[1,8]{1,0:T(1,128)} %bitcast.3), custom_call_target="tpu_custom_call" | custom-call | tf_op jit(solution)/shard_map/pallas_call | solution.py:71
  0.8 17.3 %all_to_all.10.gathered_ref = bf16[32,4,768]{2,1,0:T(4,128)(2,1)S(1)} all-to-all(bf16[32,4,768]{2,1,0:T(4,128)(2,1)S(1)} %get-tuple-element.12), channel_id=1, replica_groups={{216,88,232,104,248,120,136,8,152,24,168,40,184,56,200,72,208,80,224,96..., dimensions={0} | all-to-all | bytes 393216 | tf_op jit(solution)/shard_map/all_to_all | solution.py:238
  18.2 0.2 shard_map.38
  18.4 13.8 %all_to_all.11.pieces_ref = bf16[8,40,768]{2,1,0:T(8,128)(2,1)S(1)} all-to-all(bf16[8,40,768]{2,1,0:T(8,128)(2,1)S(1)} %shard_map.38), channel_id=1, replica_groups={{6,7,4,5,2,3,0,1},{14,10,15,11,12,8,13,9},{22,23,20,21,18,19,16,17},{30..., dimensions={0} | all-to-all | bytes 983040 | tf_op jit(solution)/shard_map/all_to_all | solution.py:239
  32.2 1.3 %collective-permute-start = (bf16[8,40,768]{2,1,0:T(8,128)(2,1)S(1)}, bf16[8,40,768]{2,1,0:T(8,128)(2,1)S(1)}, u32[]{:S(2)}, u32[]{:S(2)}) collective-permute-start(bf16[8,40,768]{2,1,0:T(8,128)(2,1)S(1)} %all_to_all.11.pieces_ref), channel_id=1, source_target_pairs={{0,8},{8,0},{1,9},{9,1},{2,10},{10,2},{3,11},{11,3},{4,12},{12,4},... | collective-permute-start | bytes 1474568 | tf_op jit(solution)/shard_map/ppermute | solution.py:240
  33.5 2.2 %shard_map.39 = (bf16[256,6400]{1,0:T(8,128)(2,1)S(1)}, f32[8,2,32,128]{3,2,1,0:T(8,128)S(1)}) custom-call(bf16[8,40,768]{2,1,0:T(8,128)(2,1)S(1)} %all_to_all.11.pieces_ref), custom_call_target="tpu_custom_call" | custom-call | flops 838860800 | bytes 4194304 | tf_op jit(solution)/shard_map/pallas_call | solution.py:241
  35.7 0.0 collective-permute-done.pieces_ref
  35.7 2.2 %shard_map.40 = f32[8,8,8,256]{3,2,1,0:T(8,128)} custom-call(bf16[8,40,768]{2,1,0:T(8,128)(2,1)S(1)} %collective-permute-done.pieces_ref, bf16[256,6400]{1,0:T(8,128)(2,1)S(1)} %get-tuple-element.13.h_ref, f32[8,2,32,128]{3,2,1,0:T(8,128)S(1)} %get-tuple-element.14.part_ref), custom_call_target="tpu_custom_call" | custom-call | flops 838860800 | bytes 4194304 | tf_op jit(solution)/shard_map/pallas_call | solution.py:250
Async XLA Ops:
  32.2 3.5 %collective-permute-start = (bf16[8,40,768]{2,1,0:T(8,128)(2,1)S(1)}, bf16[8,40,768]{2,1,0:T(8,128)(2,1)S(1)}, u32[]{:S(2)}, u32[]{:S(2)}) collective-permute-start(bf16[8,40,768]{2,1,0:T(8,128)(2,1)S(1)} %all_to_all.11.pieces_ref), channel_id=1, source_target_pairs={{0,8},{8,0},{1,9},{9,1},{2,10},{10,2},{3,11},{11,3},{4,12},{12,4},... | collective-permute-start | bytes 1474568 | tf_op jit(solution)/shard_map/ppermute | solution.py:240
